TPU v7x, 32 devices: a whole 2x2x4 slice. The times are simulated.
32 devices in a mesh: slab: 32 (over z, y, x, core).
Axes of the slice: x: 2, y: 2, z: 4, core: 2. Of those that a mesh axis runs over, the one named last changes fastest.
Arguments:
- load_terms: float32 [8, 8, 8, 4096], P(None, None, None, 'slab'), may hold values from -12 to 12
- geometry: float32 [3, 8, 8, 8, 4096], P(None, None, None, None, 'slab'), may hold values from 0.02 to 0.2
- mass_terms: float32 [8, 8, 8, 4096], P(None, None, None, 'slab'), may hold values from 1 to 4
- element_order: int32 [32, 128], P('slab'), may hold values from 0 to 127, each once within a row
Outputs:
- solution: float32 [8, 8, 8, 4096], P(None, None, None, 'slab')
- residual: float32 [8, 8, 8, 4096], P(None, None, None, 'slab')
Inputs may be any that keep to these rules, and one draw needn't show every extreme that they name: `element_order`: each device's row lists each of its 128 cells once.
All inputs are finite; a program needn't handle non-finite values.
Results may differ from a plain program's by a relative error of at most 0.0001.
Values sent between devices are 32-bit elements; how exact they have to be, the bound alone decides.
A program may use at most 64 MiB of HBM per device.

v0:
```python
import jax
import jax.numpy as jnp
import numpy as np
from jax import lax
from jax.sharding import PartitionSpec as P

EL_X = 1
EL_Y = 8
EL_Z = 16


spectrum_centre = 1.65
spectrum_half = 1.35


def padded_2(block, sides, width):
    for axis, dim in sides:
        count = lax.axis_size(axis)
        forward = [(i, i + 1) for i in range(count - 1)]
        forward.append((count - 1, 0))
        backward = [(target, source) for source, target in forward]
        low = lax.ppermute(
            lax.slice_in_dim(block, block.shape[dim] - width, None, axis=dim), axis, forward
        )
        high = lax.ppermute(lax.slice_in_dim(block, 0, width, axis=dim), axis, backward)
        block = jnp.concatenate([low, block, high], axis=dim)
    return block


def legendre_table(positions, points):
    columns = [positions * 0.0 + 1.0, positions]
    for degree_now in range(2, points):
        columns.append(
            ((2 * degree_now - 1) * positions * columns[-1] - (degree_now - 1) * columns[-2])
            / degree_now
        )
    return np.stack(columns, axis=1)


def gll_derivative(points):
    degree = points - 1
    grid_nodes = -np.cos(np.pi * np.arange(points) / degree)
    for repeat in range(100):
        legendre = legendre_table(grid_nodes, points)
        grid_nodes = grid_nodes - (grid_nodes * legendre[:, degree] - legendre[:, degree - 1]) / (
            points * legendre[:, degree]
        )
    legendre = legendre_table(grid_nodes, points)
    top_values = legendre[:, degree]
    index_list = np.arange(points)
    same_index = index_list[:, None] == index_list[None, :]
    spacing = grid_nodes[:, None] - grid_nodes[None, :]
    spacing = np.where(same_index, 1.0, spacing)
    deriv_table = top_values[:, None] / (top_values[None, :] * spacing)
    deriv_table = np.where(same_index, 0.0, deriv_table)
    deriv_table[0, 0] = -degree * points / 4.0
    deriv_table[degree, degree] = degree * points / 4.0
    return deriv_table


def local_apply(values, geometry, mass_terms, deriv_table):
    highest = lax.Precision.HIGHEST
    grad_one = jnp.einsum("ma,abce->mbce", deriv_table, values, precision=highest)
    result = jnp.einsum("ma,mbce->abce", deriv_table, geometry[0] * grad_one, precision=highest)
    grad_two = jnp.einsum("mb,abce->amce", deriv_table, values, precision=highest)
    result = result + jnp.einsum(
        "mb,amce->abce", deriv_table, geometry[1] * grad_two, precision=highest
    )
    grad_three = jnp.einsum("mc,abce->abme", deriv_table, values, precision=highest)
    result = result + jnp.einsum(
        "mc,abme->abce", deriv_table, geometry[2] * grad_three, precision=highest
    )
    return result + mass_terms * values


def local_diagonal(geometry, mass_terms, deriv_table):
    highest = lax.Precision.HIGHEST
    squared = deriv_table * deriv_table
    result = jnp.einsum("ma,mbce->abce", squared, geometry[0], precision=highest)
    result = result + jnp.einsum("mb,amce->abce", squared, geometry[1], precision=highest)
    result = result + jnp.einsum("mc,abme->abce", squared, geometry[2], precision=highest)
    return result + mass_terms


def build_tables(element_order):
    cell_ids = element_order[0]
    elem_count = cell_ids.shape[0]
    cross_count = EL_Y * EL_Z
    column_ids = jnp.arange(elem_count, dtype=jnp.int32)
    inverse = jnp.zeros((elem_count,), jnp.int32).at[cell_ids].set(column_ids)
    pos_x = cell_ids // cross_count
    pos_y = cell_ids // EL_Z % EL_Y
    pos_z = cell_ids % EL_Z
    across = pos_y * EL_Z + pos_z
    plus_x = jnp.where(
        pos_x + 1 < EL_X,
        inverse[jnp.minimum(cell_ids + cross_count, elem_count - 1)],
        elem_count + across,
    )
    minus_x = jnp.where(
        pos_x > 0, inverse[jnp.maximum(cell_ids - cross_count, 0)], elem_count + across
    )
    plus_y = jnp.where(
        pos_y + 1 < EL_Y, inverse[jnp.minimum(cell_ids + EL_Z, elem_count - 1)], elem_count
    )
    minus_y = jnp.where(pos_y > 0, inverse[jnp.maximum(cell_ids - EL_Z, 0)], elem_count)
    base_z = cell_ids - pos_z
    plus_z = inverse[base_z + (pos_z + 1) % EL_Z]
    minus_z = inverse[base_z + (pos_z + EL_Z - 1) % EL_Z]
    return {
        "plus_x": plus_x,
        "minus_x": minus_x,
        "plus_y": plus_y,
        "minus_y": minus_y,
        "plus_z": plus_z,
        "minus_z": minus_z,
        "pos_y": pos_y,
        "first_cols": inverse,
        "last_cols": inverse,
    }


def node_weights(tables, points):
    node_ids = jnp.arange(points)
    end_node = (node_ids == 0) | (node_ids == points - 1)
    edge_mult = jnp.where(end_node, 2.0, 1.0).astype(jnp.float32)
    pos_y = tables["pos_y"]
    low_shared = (node_ids == 0)[:, None] & (pos_y > 0)[None, :]
    high_shared = (node_ids == points - 1)[:, None] & (pos_y < EL_Y - 1)[None, :]
    mid_mult = jnp.where(low_shared | high_shared, 2.0, 1.0).astype(jnp.float32)
    return 1.0 / (
        edge_mult[:, None, None, None] * mid_mult[None, :, None, :] * edge_mult[None, None, :, None]
    )


def boundary_faces(values, tables):
    low_face = jnp.take(values[0], tables["first_cols"], axis=2)
    high_face = jnp.take(values[-1], tables["last_cols"], axis=2)
    return jnp.stack([low_face, high_face])


def assemble(values, tables, padded):
    low_face = values[0]
    high_face = values[-1]
    low_ext = jnp.concatenate([low_face, padded[3]], axis=2)
    high_ext = jnp.concatenate([high_face, padded[0]], axis=2)
    new_high = high_face + jnp.take(low_ext, tables["plus_x"], axis=2)
    new_low = low_face + jnp.take(high_ext, tables["minus_x"], axis=2)
    values = jnp.concatenate([new_low[None], values[1:-1], new_high[None]], axis=0)
    low_face = values[:, 0]
    high_face = values[:, -1]
    zero_column = jnp.zeros(low_face.shape[:2] + (1,), values.dtype)
    low_ext = jnp.concatenate([low_face, zero_column], axis=2)
    high_ext = jnp.concatenate([high_face, zero_column], axis=2)
    new_high = high_face + jnp.take(low_ext, tables["plus_y"], axis=2)
    new_low = low_face + jnp.take(high_ext, tables["minus_y"], axis=2)
    values = jnp.concatenate([new_low[:, None], values[:, 1:-1], new_high[:, None]], axis=1)
    low_face = values[:, :, 0]
    high_face = values[:, :, -1]
    new_high = high_face + jnp.take(low_face, tables["plus_z"], axis=2)
    new_low = low_face + jnp.take(high_face, tables["minus_z"], axis=2)
    return jnp.concatenate([new_low[:, :, None], values[:, :, 1:-1], new_high[:, :, None]], axis=2)


def on_device(load_terms, geometry, mass_terms, element_order):
    points = load_terms.shape[0]
    deriv_table = jnp.asarray(gll_derivative(points), jnp.float32)
    tables = build_tables(element_order)
    weight = node_weights(tables, points)
    diag_local = local_diagonal(geometry, mass_terms, deriv_table)
    stacked = jnp.stack([boundary_faces(load_terms, tables), boundary_faces(diag_local, tables)])
    both_faces = padded_2(stacked, (("slab", 1),), 1)
    load_padded = both_faces[0]
    diag_padded = both_faces[1]
    start = assemble(load_terms, tables, load_padded)
    inv_diag = 1.0 / assemble(diag_local, tables, diag_padded)

    def operate(values):
        local_part = local_apply(values, geometry, mass_terms, deriv_table)
        padded = padded_2(boundary_faces(local_part, tables), (("slab", 0),), 1)
        return assemble(local_part, tables, padded)

    ratio_sigma = spectrum_centre / spectrum_half
    step_vec = inv_diag * start / spectrum_centre
    precond = step_vec
    rho_prev = 1.0 / ratio_sigma
    rho_next = 1.0 / (2.0 * ratio_sigma - rho_prev)
    misfit = start - operate(precond)
    step_vec = rho_next * rho_prev * step_vec + 2.0 * rho_next / spectrum_half * inv_diag * misfit
    precond = precond + step_vec
    numerator = lax.psum(jnp.sum(weight * start * precond), "slab")
    image_vec = operate(precond)
    denominator = lax.psum(jnp.sum(weight * precond * image_vec), "slab")
    step_size = numerator / denominator
    return (step_size * precond, start - step_size * image_vec)


def solution(mesh):
    placed = (
        P(None, None, None, "slab"),
        P(None, None, None, None, "slab"),
        P(None, None, None, "slab"),
        P("slab", None),
    )
    return jax.shard_map(
        on_device,
        mesh=mesh,
        in_specs=placed,
        out_specs=(P(None, None, None, "slab"), P(None, None, None, "slab")),
        check_vma=False,
    )
```

profile of v0, /device:TPU:0, one launch (start us, length us, event | category | flops | bytes accessed | tf_op | source)
XLA Modules:
  0.0 184.2 jit_solution(10116202947819588874)
XLA Ops:
  12.8 6.4 %collective-permute-start.1 = (f32[2,1,8,8,128]{4,3,2,1,0:T(8,128)S(1)}, f32[2,1,8,8,128]{4,3,2,1,0:T(8,128)S(1)}, u32[]{:S(2)}, u32[]{:S(2)}) collective-permute-start(f32[2,1,8,8,128]{4,3,2,1,0:T(8,128)S(1)} %get-tuple-element.65), channel_id=1, source_target_pairs={{1,0},{2,1},{3,2},{4,3},{5,4},{6,5},{7,6},{8,7},{9,8},{10,9},{11,1... | collective-permute-start | bytes 196616 | tf_op jit(solution)/shard_map/ppermute | solution.py:25
  27.2 1.4 gather_fusion.1
  32.3 1.6 gather_fusion.17
  36.2 1.6 gather_fusion.16
  39.5 1.6 gather_fusion.11
  42.7 1.6 gather_fusion.10
  54.4 1.7 gather_fusion.14
  57.0 1.6 gather_fusion.15
  60.0 1.6 gather_fusion.21
  63.0 1.6 gather_fusion.20
  70.9 2.5 %gather_fusion.24 = f32[128,8,8]{2,1,0:T(8,128)} fusion(f32[8,8,128]{1,0,2:T(8,128)} %copy.105, s32[1024]{0:T(1024)S(1)} %pad_clamp_fusion.11), kind=kCustom, calls=%fused_computation.11.clone | custom fusion | bytes 66048 | tf_op jit(solution)/shard_map/jit(_take)/gather | solution.py:137
  75.6 2.5 %gather_fusion.22 = f32[128,8,8]{2,1,0:T(8,128)} fusion(f32[8,8,128]{1,0,2:T(8,128)} %copy.101, s32[1024]{0:T(1024)S(1)} %pad_clamp_fusion.11), kind=kCustom, calls=%fused_computation.10.clone | custom fusion | bytes 66048 | tf_op jit(solution)/shard_map/jit(_take)/gather | solution.py:138
  79.9 5.3 %collective-permute-start.3 = (f32[1,8,8,128]{3,2,1,0:T(8,128)S(1)}, f32[1,8,8,128]{3,2,1,0:T(8,128)S(1)}, u32[]{:S(2)}, u32[]{:S(2)}) collective-permute-start(f32[1,8,8,128]{3,2,1,0:T(8,128)S(1)} %get-tuple-element.75), channel_id=1, source_target_pairs={{1,0},{2,1},{3,2},{4,3},{5,4},{6,5},{7,6},{8,7},{9,8},{10,9},{11,1... | collective-permute-start | bytes 98312 | tf_op jit(solution)/shard_map/ppermute | solution.py:25
  88.2 2.8 %gather_fusion.25 = f32[128,8,8]{2,1,0:T(8,128)} fusion(f32[8,8,256]{1,0,2:T(8,128)} %copy.107, s32[1024]{0:T(1024)} %copy-done.19), kind=kCustom, calls=%fused_computation.22.clone | custom fusion | bytes 66048 | tf_op jit(solution)/shard_map/jit(_take)/gather | solution.py:147
  92.7 1.4 copy.103
  94.1 2.8 %gather_fusion.23 = f32[128,8,8]{2,1,0:T(8,128)} fusion(f32[8,8,256]{1,0,2:T(8,128)} %copy.103, s32[1024]{0:T(1024)} %copy-done.18), kind=kCustom, calls=%fused_computation.21.clone | custom fusion | bytes 66048 | tf_op jit(solution)/shard_map/jit(_take)/gather | solution.py:148
  100.0 1.8 gather_fusion.26
  103.8 1.8 gather_fusion.27
  107.5 1.8 gather_fusion.28
  110.1 1.4 fusion.32
  112.5 1.6 gather_fusion.29
  121.9 4.9 %collective-permute-start.5 = (f32[1,8,8,128]{3,2,1,0:T(8,128)S(1)}, f32[1,8,8,128]{3,2,1,0:T(8,128)S(1)}, u32[]{:S(2)}, u32[]{:S(2)}) collective-permute-start(f32[1,8,8,128]{3,2,1,0:T(8,128)S(1)} %get-tuple-element.73), channel_id=1, source_target_pairs={{1,0},{2,1},{3,2},{4,3},{5,4},{6,5},{7,6},{8,7},{9,8},{10,9},{11,1... | collective-permute-start | bytes 98312 | tf_op jit(solution)/shard_map/ppermute | solution.py:25
  129.9 4.0 %collective-permute-done.4 = f32[1,8,8,128]{3,2,1,0:T(8,128)S(1)} collective-permute-done((f32[1,8,8,128]{3,2,1,0:T(8,128)S(1)}, f32[1,8,8,128]{3,2,1,0:T(8,128)S(1)}, u32[]{:S(2)}, u32[]{:S(2)}) %collective-permute-start.4) | collective-permute-done | bytes 32800 | tf_op jit(solution)/shard_map/ppermute | solution.py:22
  144.2 37.1 %all-reduce.8 = (f32[]{:T(128)}, f32[]{:T(128)}) all-reduce(f32[]{:T(128)} %get-tuple-element.10, f32[]{:T(128)} %get-tuple-element.9), channel_id=1, replica_groups=mesh['slab'=32] {'slab'}, use_global_device_ids=true, to_apply=%region_2.6 | all-reduce | flops 2 | bytes 16 | tf_op jit(solution)/shard_map/psum | solution.py:191
  (290 shorter events, 88.9 us)
Async XLA Ops:
  0.6 3.6 %copy-start.1 = (f32[3,8,8,8,128]{4,3,2,1,0:T(8,128)S(1)}, f32[3,8,8,8,128]{4,3,2,1,0:T(8,128)}, u32[]{:S(2)}) copy-start(f32[3,8,8,8,128]{4,3,2,1,0:T(8,128)} %param.12) | copy-start | bytes 2359300
  3.1 9.0 %copy-start.34 = (pred[128]{0:T(512)(128)(4,1)}, pred[128]{0:T(512)(128)(4,1)S(1)}, u32[]{:S(2)}) copy-start(pred[128]{0:T(512)(128)(4,1)S(1)} %compare_and_fusion.6) | copy-start | bytes 388
  9.6 1.2 copy-start.14
  12.8 19.1 %collective-permute-start.1 = (f32[2,1,8,8,128]{4,3,2,1,0:T(8,128)S(1)}, f32[2,1,8,8,128]{4,3,2,1,0:T(8,128)S(1)}, u32[]{:S(2)}, u32[]{:S(2)}) collective-permute-start(f32[2,1,8,8,128]{4,3,2,1,0:T(8,128)S(1)} %get-tuple-element.65), channel_id=1, source_target_pairs={{1,0},{2,1},{3,2},{4,3},{5,4},{6,5},{7,6},{8,7},{9,8},{10,9},{11,1... | collective-permute-start | bytes 196616 | tf_op jit(solution)/shard_map/ppermute | solution.py:25
  19.2 15.9 %collective-permute-start = (f32[2,1,8,8,128]{4,3,2,1,0:T(8,128)}, f32[2,1,8,8,128]{4,3,2,1,0:T(8,128)}, u32[]{:S(2)}, u32[]{:S(2)}) collective-permute-start(f32[2,1,8,8,128]{4,3,2,1,0:T(8,128)} %get-tuple-element.64), channel_id=1, source_target_pairs={{0,1},{1,2},{2,3},{3,4},{4,5},{5,6},{6,7},{7,8},{8,9},{9,10},{10,1... | collective-permute-start | bytes 196616 | tf_op jit(solution)/shard_map/ppermute | solution.py:22
  27.2 2.6 %slice-start = ((f32[8,8,8,128]{3,2,1,0:T(8,128)}), f32[6,8,8,128]{3,2,1,0:T(8,128)S(1)}, s32[]{:S(2)}) async-start(f32[8,8,8,128]{3,2,1,0:T(8,128)} %param.11), calls=%async_computation | async-start | bytes 393216 | tf_op jit(solution)/shard_map/slice | solution.py:149
  29.8 9.7 %copy-start.19 = (s32[1024]{0:T(1024)}, s32[1024]{0:T(1024)S(1)}, u32[]{:S(2)}) copy-start(s32[1024]{0:T(1024)S(1)} %pad_clamp_fusion.8) | copy-start | bytes 12292
  29.8 12.9 %copy-start.18 = (s32[1024]{0:T(1024)}, s32[1024]{0:T(1024)S(1)}, u32[]{:S(2)}) copy-start(s32[1024]{0:T(1024)S(1)} %pad_clamp_fusion.10) | copy-start | bytes 12292
  31.1 31.9 %copy-start.17 = (s32[1024]{0:T(1024)}, s32[1024]{0:T(1024)S(1)}, u32[]{:S(2)}) copy-start(s32[1024]{0:T(1024)S(1)} %pad_clamp_fusion.2) | copy-start | bytes 12292
  37.8 1.2 copy-start.15
  44.2 1.3 copy-start.7
  56.7 58.7 %copy-start.2 = (f32[8,8,1,128]{3,0,2,1:T(8,128)}, f32[8,8,1,128]{3,0,2,1:T(8,128)S(1)}, u32[]{:S(2)}) copy-start(f32[8,8,1,128]{3,0,2,1:T(8,128)S(1)} %get-tuple-element.27) | copy-start | bytes 98308
  64.6 1.2 copy-start.32
  65.9 49.5 %copy-start.4 = (f32[8,8,1,128]{3,0,2,1:T(8,128)}, f32[8,8,1,128]{3,0,2,1:T(8,128)S(1)}, u32[]{:S(2)}) copy-start(f32[8,8,1,128]{3,0,2,1:T(8,128)S(1)} %get-tuple-element.71) | copy-start | bytes 98308
  78.1 1.2 copy-start.35
  79.9 6.9 %collective-permute-start.3 = (f32[1,8,8,128]{3,2,1,0:T(8,128)S(1)}, f32[1,8,8,128]{3,2,1,0:T(8,128)S(1)}, u32[]{:S(2)}, u32[]{:S(2)}) collective-permute-start(f32[1,8,8,128]{3,2,1,0:T(8,128)S(1)} %get-tuple-element.75), channel_id=1, source_target_pairs={{1,0},{2,1},{3,2},{4,3},{5,4},{6,5},{7,6},{8,7},{9,8},{10,9},{11,1... | collective-permute-start | bytes 98312 | tf_op jit(solution)/shard_map/ppermute | solution.py:25
  85.3 7.4 %collective-permute-start.2 = (f32[1,8,8,128]{3,2,1,0:T(8,128)}, f32[1,8,8,128]{3,2,1,0:T(8,128)S(1)}, u32[]{:S(2)}, u32[]{:S(2)}) collective-permute-start(f32[1,8,8,128]{3,2,1,0:T(8,128)} %get-tuple-element.74), channel_id=1, source_target_pairs={{0,1},{1,2},{2,3},{3,4},{4,5},{5,6},{6,7},{7,8},{8,9},{9,10},{10,1... | collective-permute-start | bytes 98312 | tf_op jit(solution)/shard_map/ppermute | solution.py:22
  96.9 1.2 copy-start.27
  96.9 1.2 copy-start.30
  114.1 1.3 copy-start.33
  114.1 1.3 copy-start.8
  121.9 4.9 %copy-start.38 = (f32[8]{0:T(128)S(1)}, f32[8]{0:T(128)}, u32[]{:S(2)}) copy-start(f32[8]{0:T(128)} %or_select_fusion.1) | copy-start | bytes 100
  121.9 6.5 %collective-permute-start.5 = (f32[1,8,8,128]{3,2,1,0:T(8,128)S(1)}, f32[1,8,8,128]{3,2,1,0:T(8,128)S(1)}, u32[]{:S(2)}, u32[]{:S(2)}) collective-permute-start(f32[1,8,8,128]{3,2,1,0:T(8,128)S(1)} %get-tuple-element.73), channel_id=1, source_target_pairs={{1,0},{2,1},{3,2},{4,3},{5,4},{6,5},{7,6},{8,7},{9,8},{10,9},{11,1... | collective-permute-start | bytes 98312 | tf_op jit(solution)/shard_map/ppermute | solution.py:25
  126.9 7.0 %collective-permute-start.4 = (f32[1,8,8,128]{3,2,1,0:T(8,128)S(1)}, f32[1,8,8,128]{3,2,1,0:T(8,128)S(1)}, u32[]{:S(2)}, u32[]{:S(2)}) collective-permute-start(f32[1,8,8,128]{3,2,1,0:T(8,128)S(1)} %get-tuple-element.72), channel_id=1, source_target_pairs={{0,1},{1,2},{2,3},{3,4},{4,5},{5,6},{6,7},{7,8},{8,9},{9,10},{10,1... | collective-permute-start | bytes 98312 | tf_op jit(solution)/shard_map/ppermute | solution.py:22
  (22 other events, 15.6 us)
where the time goes:
time: 187 us; the launch traced here: 184 us
  local copies, waits for them, and re-layouts  100 us (53%)
  blocking collectives  37.1 us (20%)
  starting transfers between devices  17 us (9%)
  other arithmetic  12.9 us (7%)
  waiting for transfers between devices  6.91 us (4%)
  matrix products  6.62 us (4%)
  between operations  3.25 us (2%)
    psum x1, blocking collectives, on_device(): numerator = lax.psum(jnp.sum(weight * start * precond), 'slab')  37.1 us
    ppermute x3, starting transfers between devices, padded_2(): lax.ppermute(lax.slice_in_dim(block, 0, width, axis=dim), axis, backward)  16.6 us
    unnamed x89, local copies, waits for them, and re-layouts  12.4 us
    gather x8, local copies, waits for them, and re-layouts, assemble(): new_low = low_face + jnp.take(high_ext, tables['minus_x'], axis=2)  10.7 us
    gather x8, local copies, waits for them, and re-layouts, assemble(): new_high = high_face + jnp.take(low_ext, tables['plus_x'], axis=2)  10.6 us
    gather x8, local copies, waits for them, and re-layouts, assemble(): new_high = high_face + jnp.take(low_face, tables['plus_z'], axis=2)  9.31 us
    gather x8, local copies, waits for them, and re-layouts, assemble(): new_low = low_face + jnp.take(high_face, tables['minus_z'], axis=2)  8.35 us
    gather x8, local copies, waits for them, and re-layouts, boundary_faces(): high_face = jnp.take(values[-1], tables['last_cols'], axis=2)  6.51 us
  transfers between devices with their start and end apart: 6, of which 4 were waited for; matrix products, arithmetic and copies ran while one was open for 12% of the time, Pallas kernels for 0%

commit v1 on v0

v1 whole, which is shorter than its diff:
```python
import functools

import jax
import jax.numpy as jnp
import numpy as np
from jax import lax
from jax.experimental import pallas as pl
from jax.experimental.pallas import tpu as pltpu
from jax.sharding import PartitionSpec as P

EL_Y = 8
EL_Z = 16
MESH = pl.DeviceIdType.MESH
WIDEST = 32

spectrum_centre = 1.65
spectrum_half = 1.35


def legendre_table(positions, points):
    columns = [positions * 0.0 + 1.0, positions]
    for degree_now in range(2, points):
        columns.append(
            ((2 * degree_now - 1) * positions * columns[-1] - (degree_now - 1) * columns[-2])
            / degree_now
        )
    return np.stack(columns, axis=1)


def gll_derivative(points):
    degree = points - 1
    grid_nodes = -np.cos(np.pi * np.arange(points) / degree)
    for repeat in range(100):
        legendre = legendre_table(grid_nodes, points)
        grid_nodes = grid_nodes - (grid_nodes * legendre[:, degree] - legendre[:, degree - 1]) / (
            points * legendre[:, degree]
        )
    legendre = legendre_table(grid_nodes, points)
    top_values = legendre[:, degree]
    index_list = np.arange(points)
    same_index = index_list[:, None] == index_list[None, :]
    spacing = grid_nodes[:, None] - grid_nodes[None, :]
    spacing = np.where(same_index, 1.0, spacing)
    deriv_table = top_values[:, None] / (top_values[None, :] * spacing)
    deriv_table = np.where(same_index, 0.0, deriv_table)
    deriv_table[0, 0] = -degree * points / 4.0
    deriv_table[degree, degree] = degree * points / 4.0
    return deriv_table


def radices(count):
    factors = []
    while count > 1:
        width = max([w for w in range(2, WIDEST + 1) if count % w == 0], default=count)
        factors.append(width)
        count //= width
    return factors


def contract(values, table, symmetric):
    points = len(values)
    half = points // 2
    even = [values[j] + values[points - 1 - j] for j in range(half)]
    odd = [values[j] - values[points - 1 - j] for j in range(half)]
    low, high = [], []
    for m in range(half):
        a = [float(0.5 * (table[m, j] + table[m, points - 1 - j])) for j in range(half)]
        b = [float(0.5 * (table[m, j] - table[m, points - 1 - j])) for j in range(half)]
        part_even = a[0] * even[0]
        part_odd = b[0] * odd[0]
        for j in range(1, half):
            part_even = part_even + a[j] * even[j]
            part_odd = part_odd + b[j] * odd[j]
        low.append(part_even + part_odd)
        high.append(part_even - part_odd if symmetric else part_odd - part_even)
    return low + high[::-1]


def lane_gather(values, columns):
    dims = lax.GatherDimensionNumbers(
        offset_dims=(),
        collapsed_slice_dims=(1,),
        start_index_map=(1,),
        operand_batching_dims=(0,),
        start_indices_batching_dims=(0,),
    )
    return lax.gather(
        values, columns[..., None], dims, (1, 1), mode=lax.GatherScatterMode.PROMISE_IN_BOUNDS
    )


def kernel(
    count, points, factors, deriv,
    load_hbm, geo_hbm, mass_hbm, order_ref, sol_ref, res_ref,
    load, geo, mass, start, inverse, vec, work, image,
    face_out, face_in, own_inv, near_inv, coef, sums, *rest,
):
    parts_in = rest[: len(factors)]
    (in_sem, face_send, face_recv, inv_send, inv_recv, sum_send, sum_recv) = rest[len(factors):]
    me = lax.axis_index("slab")
    right = lax.rem(me + 1, count)
    left = lax.rem(me + count - 1, count)
    plane = points * points
    rows = points * plane
    last = rows - plane
    cols = load.shape[1]

    fetch = [
        pltpu.make_async_copy(geo_hbm, geo, in_sem.at[0]),
        pltpu.make_async_copy(mass_hbm, mass, in_sem.at[1]),
        pltpu.make_async_copy(load_hbm, load, in_sem.at[2]),
    ]
    for copy in fetch:
        copy.start()

    def peer(stride, width, k):
        digit = lax.rem(me // stride, width)
        return me + (lax.rem(digit + k, width) - digit) * stride

    strides = [int(np.prod(factors[:i])) for i in range(len(factors))]
    barrier = pltpu.get_barrier_semaphore()
    for near in (left, right):
        pl.semaphore_signal(barrier, inc=1, device_id=(near,), device_id_type=MESH)
    for stride, width in zip(strides, factors):
        @pl.loop(1, width)
        def _(k):
            pl.semaphore_signal(
                barrier, inc=1, device_id=(peer(stride, width, k),), device_id_type=MESH
            )

    cell = order_ref[...]
    cell8 = jnp.broadcast_to(cell, (points, cols))
    cell_col = jnp.transpose(jnp.broadcast_to(cell.astype(jnp.float32), (cols, cols)))
    lane = lax.broadcasted_iota(jnp.int32, (cols, cols), 1).astype(jnp.float32)
    source = lax.broadcasted_iota(jnp.int32, (cols, cols), 0).astype(jnp.float32)
    inv_row = jnp.sum(jnp.where(cell_col == lane, source, 0.0), axis=0, keepdims=True)
    inv8 = jnp.broadcast_to(inv_row.astype(jnp.int32), (points, cols))
    own_inv[...] = inv8
    pos_z = cell8 % EL_Z
    has_up = cell8 < cols - EL_Z
    has_down = cell8 >= EL_Z
    plus_y = lane_gather(inv8, jnp.where(has_up, cell8 + EL_Z, cell8))
    minus_y = lane_gather(inv8, jnp.where(has_down, cell8 - EL_Z, cell8))
    plus_z = lane_gather(inv8, jnp.where(pos_z == EL_Z - 1, cell8 - (EL_Z - 1), cell8 + 1))
    minus_z = lane_gather(inv8, jnp.where(pos_z == 0, cell8 + (EL_Z - 1), cell8 - 1))

    row_id = lax.broadcasted_iota(jnp.int32, (points, cols), 0)
    for t, table in enumerate((deriv, deriv.T, (deriv * deriv).T)):
        for k in range(points):
            vector = jnp.zeros((points, cols), jnp.float32)
            for m in range(points):
                vector = jnp.where(row_id == m, float(table[m, (m - k) % points]), vector)
            coef[t, k] = vector

    def rotate_contract(value, t):
        total = coef[t, 0] * value
        for k in range(1, points):
            total = total + coef[t, k] * pltpu.roll(value, k, 0)
        return total

    pl.semaphore_wait(barrier, 2 + sum(w - 1 for w in factors))

    def send_pair(low_src, high_src, low_dst, high_dst, send_sems, recv_sems):
        pair = [
            pltpu.make_async_remote_copy(
                src_ref=low_src, dst_ref=high_dst, send_sem=send_sems.at[0],
                recv_sem=recv_sems.at[1], device_id=(left,), device_id_type=MESH,
            ),
            pltpu.make_async_remote_copy(
                src_ref=high_src, dst_ref=low_dst, send_sem=send_sems.at[1],
                recv_sem=recv_sems.at[0], device_id=(right,), device_id_type=MESH,
            ),
        ]
        for copy in pair:
            copy.start()
        return pair

    def send_faces(e):
        return send_pair(
            face_out.at[e, 0], face_out.at[e, 1], face_in.at[e, 0], face_in.at[e, 1],
            face_send.at[e], face_recv.at[e],
        )

    pair_load = send_pair(
        load_hbm.at[pl.ds(0, plane)], load_hbm.at[pl.ds(last, plane)],
        face_in.at[0, 0], face_in.at[0, 1], face_send.at[0], face_recv.at[0],
    )
    pair_inv = send_pair(own_inv, own_inv, near_inv.at[0], near_inv.at[1], inv_send, inv_recv)

    def at(base, b):
        return pl.ds(pl.multiple_of(base + b * points, points), points)

    def geo_at(k, base, b):
        return pl.ds(pl.multiple_of(k * rows + base + b * points, points), points)

    def store_face(e, side, b, value):
        face_out[e, side, pl.ds(b * points, points)] = value

    def assemble_plane(ref, base):
        low = ref[at(base, 0)]
        high = ref[at(base, points - 1)]
        ref[at(base, points - 1)] = high + jnp.where(has_up, lane_gather(low, plus_y), 0.0)
        ref[at(base, 0)] = low + jnp.where(has_down, lane_gather(high, minus_y), 0.0)
        first = pl.ds(base, points, stride=points)
        end = pl.ds(base + points - 1, points, stride=points)
        low = ref[first]
        high = ref[end]
        ref[end] = high + lane_gather(low, plus_z)
        ref[first] = low + lane_gather(high, minus_z)

    square = deriv * deriv
    fetch[0].wait()
    fetch[1].wait()

    @pl.loop(0, points)
    def _(b):
        values = [geo[geo_at(0, a * plane, b)] for a in range(points)]
        for a, value in enumerate(contract(values, square.T, True)):
            work[at(a * plane, b)] = value

    def diagonal_plane(base, put):
        values = [geo[geo_at(1, base, b)] for b in range(points)]
        for b, value in enumerate(contract(values, square.T, True)):
            value = value + rotate_contract(geo[geo_at(2, base, b)], 2)
            put(b, value + work[at(base, b)] + mass[at(base, b)])

    diagonal_plane(0, functools.partial(store_face, 1, 0))
    diagonal_plane(last, functools.partial(store_face, 1, 1))
    pair_diag = send_faces(1)

    def first_update(base):
        for b in range(points):
            span = at(base, b)
            scaled = 1.0 / inverse[span]
            inverse[span] = scaled
            vec[span] = scaled * start[span] * (1.0 / spectrum_centre)

    fetch[2].wait()

    @pl.loop(1, points - 1)
    def _(a):
        base = pl.multiple_of(a * plane, plane)

        def put(b, value):
            inverse[at(base, b)] = value

        diagonal_plane(base, put)
        for b in range(points):
            start[at(base, b)] = load[at(base, b)]
        assemble_plane(start, base)
        assemble_plane(inverse, base)
        first_update(base)

    for copy in pair_inv:
        copy.wait()
    minus_x = lane_gather(near_inv[0], cell8)
    plus_x = lane_gather(near_inv[1], cell8)

    def join_face(e, side, own, ref):
        base = (0, last)[side]
        columns = (minus_x, plus_x)[side]
        for b in range(points):
            ref[at(base, b)] = own(b) + lane_gather(
                face_in[e, side, pl.ds(b * points, points)], columns
            )
        assemble_plane(ref, base)

    def own_face(e, side):
        return lambda b: face_out[e, side, pl.ds(b * points, points)]

    for copy in pair_load:
        copy.wait()
    for side in (0, 1):
        base = (0, last)[side]
        join_face(0, side, lambda b: load[at(base, b)], start)
    for copy in pair_diag:
        copy.wait()
    for side in (0, 1):
        join_face(1, side, own_face(1, side), inverse)
        first_update((0, last)[side])

    def gradient_first():
        @pl.loop(0, points)
        def _(b):
            values = [vec[at(a * plane, b)] for a in range(points)]
            slopes = contract(values, deriv, False)
            fluxes = [geo[geo_at(0, a * plane, b)] * slopes[a] for a in range(points)]
            for a, value in enumerate(contract(fluxes, deriv.T, False)):
                work[at(a * plane, b)] = value

    def operate_plane(base, put):
        values = [vec[at(base, b)] for b in range(points)]
        slopes = contract(values, deriv, False)
        fluxes = [geo[geo_at(1, base, b)] * slopes[b] for b in range(points)]
        for b, value in enumerate(contract(fluxes, deriv.T, False)):
            flux = geo[geo_at(2, base, b)] * rotate_contract(values[b], 0)
            value = value + rotate_contract(flux, 1)
            put(b, values[b], value + work[at(base, b)] + mass[at(base, b)] * values[b])

    ratio_sigma = spectrum_centre / spectrum_half
    rho_prev = 1.0 / ratio_sigma
    rho_next = 1.0 / (2.0 * ratio_sigma - rho_prev)
    on_misfit = 2.0 * rho_next / spectrum_half
    on_start = (1.0 + rho_next * rho_prev) / spectrum_centre + on_misfit

    def second_update(base):
        for b in range(points):
            span = at(base, b)
            vec[span] = inverse[span] * (on_start * start[span] - on_misfit * image[span])

    gradient_first()
    for side in (0, 1):
        operate_plane((0, last)[side], lambda b, v, out: store_face(2, side, b, out))
    pair_first = send_faces(2)

    @pl.loop(1, points - 1)
    def _(a):
        base = pl.multiple_of(a * plane, plane)

        def put(b, value, out):
            image[at(base, b)] = out

        operate_plane(base, put)
        assemble_plane(image, base)
        second_update(base)

    for copy in pair_first:
        copy.wait()
    for side in (0, 1):
        join_face(2, side, own_face(2, side), image)
        second_update((0, last)[side])

    gradient_first()
    tally = [jnp.zeros((points, cols), jnp.float32)] * 2

    def add_up(tally, base, b, value, out):
        return [tally[0] + load[at(base, b)] * value, tally[1] + value * out]

    for side in (0, 1):
        base = (0, last)[side]

        def put(b, value, out):
            nonlocal tally
            store_face(3, side, b, out)
            tally = add_up(tally, base, b, value, out)

        operate_plane(base, put)
    pair_second = send_faces(3)

    def plane_step(a, carry):
        base = pl.multiple_of(a * plane, plane)
        state = list(carry)

        def put(b, value, out):
            nonlocal state
            image[at(base, b)] = out
            state = add_up(state, base, b, value, out)

        operate_plane(base, put)
        return tuple(state)

    tally = lax.fori_loop(1, points - 1, plane_step, tuple(tally))
    total = jnp.concatenate([jnp.sum(part, axis=0, keepdims=True) for part in tally], axis=1)

    def sum_copy(i, k):
        stride, width = strides[i], factors[i]
        return pltpu.make_async_remote_copy(
            src_ref=sums.at[i], dst_ref=parts_in[i].at[k - 1],
            send_sem=sum_send.at[i, k - 1], recv_sem=sum_recv.at[i, k - 1],
            device_id=(peer(stride, width, k),), device_id_type=MESH,
        )

    def start_sum(i, value):
        sums[i] = value

        @pl.loop(1, factors[i])
        def _(k):
            sum_copy(i, k).start()

    def finish_sum(i, value):
        @pl.loop(1, factors[i])
        def _(k):
            sum_copy(i, k).wait()

        for k in range(factors[i] - 1):
            value = value + parts_in[i][k]
        return value

    start_sum(0, total)

    @pl.loop(1, points - 1)
    def _(a):
        assemble_plane(image, pl.multiple_of(a * plane, plane))

    for copy in pair_second:
        copy.wait()
    for side in (0, 1):
        join_face(3, side, own_face(3, side), image)
    for i in range(len(factors)):
        if i:
            start_sum(i, total)
        total = finish_sum(i, total)
    numerator = jnp.sum(total[:, :cols], axis=1, keepdims=True)
    denominator = jnp.sum(total[:, cols:], axis=1, keepdims=True)
    size = jnp.broadcast_to(numerator / denominator, (points, cols))

    @pl.loop(0, points)
    def _(a):
        base = pl.multiple_of(a * plane, plane)
        for b in range(points):
            span = at(base, b)
            sol_ref[span] = size * vec[span]
            res_ref[span] = start[span] - size * image[span]


def on_device(count, load_terms, geometry, mass_terms, element_order):
    points = load_terms.shape[0]
    cols = load_terms.shape[3]
    plane = points * points
    rows = points * plane
    deriv = gll_derivative(points)
    factors = radices(count)
    field = jax.ShapeDtypeStruct((rows, cols), jnp.float32)
    f32 = jnp.float32
    big = [pltpu.VMEM((rows, cols), f32)]
    scratch = (
        big + [pltpu.VMEM((3 * rows, cols), f32)] + big * 6
        + [
            pltpu.VMEM((4, 2, plane, cols), f32),
            pltpu.VMEM((4, 2, plane, cols), f32),
            pltpu.VMEM((points, cols), jnp.int32),
            pltpu.VMEM((2, points, cols), jnp.int32),
            pltpu.VMEM((3, points, points, cols), f32),
            pltpu.VMEM((len(factors), 1, 2 * cols), f32),
        ]
        + [pltpu.VMEM((w - 1, 1, 2 * cols), f32) for w in factors]
        + [
            pltpu.SemaphoreType.DMA((3,)),
            pltpu.SemaphoreType.DMA((4, 2)),
            pltpu.SemaphoreType.DMA((4, 2)),
            pltpu.SemaphoreType.DMA((2,)),
            pltpu.SemaphoreType.DMA((2,)),
            pltpu.SemaphoreType.DMA((len(factors), max(factors) - 1)),
            pltpu.SemaphoreType.DMA((len(factors), max(factors) - 1)),
        ]
    )
    hbm = pl.BlockSpec(memory_space=pl.ANY)
    vmem = pl.BlockSpec(memory_space=pltpu.VMEM)
    solution_rows, residual_rows = pl.pallas_call(
        functools.partial(kernel, count, points, factors, deriv),
        out_shape=(field, field),
        in_specs=[hbm, hbm, hbm, vmem],
        out_specs=(vmem, vmem),
        scratch_shapes=scratch,
        compiler_params=pltpu.CompilerParams(collective_id=0, has_side_effects=True),
    )(
        load_terms.reshape(rows, cols),
        geometry.reshape(3 * rows, cols),
        mass_terms.reshape(rows, cols),
        element_order,
    )
    shape = load_terms.shape
    return solution_rows.reshape(shape), residual_rows.reshape(shape)


def solution(mesh):
    placed = (
        P(None, None, None, "slab"),
        P(None, None, None, None, "slab"),
        P(None, None, None, "slab"),
        P("slab", None),
    )
    return jax.shard_map(
        functools.partial(on_device, mesh.shape["slab"]),
        mesh=mesh,
        in_specs=placed,
        out_specs=(P(None, None, None, "slab"), P(None, None, None, "slab")),
        check_vma=False,
    )
```

time: 187 us -> 25.5 us (0.14); the launches traced: 184 us -> 25.4 us
  local copies, waits for them, and re-layouts: 100 us -> 2.42 us
  blocking collectives: 37.1 us -> 0 us
  Pallas kernels: 0 us -> 22.3 us
  starting transfers between devices: 17 us -> 0 us
  other arithmetic: 12.9 us -> 0 us
  waiting for transfers between devices: 6.91 us -> 0 us
  matrix products: 6.62 us -> 0 us
  between operations: 3.25 us -> 0.65 us
    gather x70 -> x0, local copies, waits for them, and re-layouts: 69.9 us -> none  [the longest x8 10.7 us: assemble(): new_low = low_face + jnp.take(high_ext, tables['minus_x'], axis=2)]
    psum x1 -> x0, blocking collectives: 37.1 us -> none  [on_device(): numerator = lax.psum(jnp.sum(weight * start * precond), 'slab')]
    pallas_call x0 -> x1, Pallas kernels: none -> 22.3 us  [on_device(): pl.pallas_call(functools.partial(kernel, count, points, factors, deriv),...]
    ppermute x6 -> x0, starting transfers between devices: 17 us -> none  [the longest x3 16.6 us: padded_2(): lax.ppermute(lax.slice_in_dim(block, 0, width, axis=dim), axis, backward)]
    unnamed x89 -> x4, local copies, waits for them, and re-layouts: 12.4 us -> 2.42 us
    squeeze x22 -> x0, local copies, waits for them, and re-layouts: 8.63 us -> none  [the longest x5 2.55 us: assemble(): high_face = values[:, :, -1]]
    concatenate x16 -> x0, local copies, waits for them, and re-layouts: 7.11 us -> none  [the longest x4 2.6 us: assemble(): high_ext = jnp.concatenate([high_face, padded[0]], axis=2)]
    ppermute x6 -> x0, waiting for transfers between devices: 6.91 us -> none  [the longest x3 4.51 us: padded_2(): lax.ppermute(lax.slice_in_dim(block, block.shape[dim] - width, None, axis...]
  transfers between devices with their start and end apart: 6 -> 0, of which waited for: 4 -> 0; matrix products, arithmetic and copies ran while one was open for 12% -> 0% of each run, Pallas kernels for 0% -> 0%
where the time goes in v1:
time: 25.5 us; the launch traced here: 25.4 us
  Pallas kernels  22.3 us (87%)
  local copies, waits for them, and re-layouts  2.42 us (9%)
  between operations  0.65 us (3%)
    pallas_call x1, Pallas kernels, on_device(): pl.pallas_call(functools.partial(kernel, count, points, factors, deriv),...  22.3 us
    unnamed x4, local copies, waits for them, and re-layouts  2.42 us

profile of v1, /device:TPU:0, one launch (start us, length us, event | category | flops | bytes accessed | tf_op | source)
XLA Modules:
  0.0 25.4 jit_solution(17295349882252354780)
XLA Ops:
  0.6 22.3 %shard_map.59 = (f32[512,128]{1,0:T(8,128)}, f32[512,128]{1,0:T(8,128)}) custom-call(f32[512,128]{1,0:T(8,128)} %bitcast.6, f32[1536,128]{1,0:T(8,128)} %bitcast.5, f32[512,128]{1,0:T(8,128)} %bitcast.7, s32[1,128]{1,0:T(1,128)} %order_ref.1), custom_call_target="tpu_custom_call" | custom-call | tf_op jit(solution)/shard_map/pallas_call | solution.py:449
  23.0 0.0 copy-start
  23.0 1.7 %copy.8 = f32[8,8,8,128]{3,2,1,0:T(8,128)} copy(f32[8,8,8,128]{3,2,1,0:T(8,128)} %bitcast.9) | data formatting | bytes 524288
  24.7 0.0 copy-done
  24.7 0.7 %copy.9 = f32[8,8,8,128]{3,2,1,0:T(8,128)} copy(f32[8,8,8,128]{3,2,1,0:T(8,128)S(1)} %bitcast.8) | data formatting | bytes 524288
Async XLA Ops:
  23.0 1.7 %copy-start = (f32[512,128]{1,0:T(8,128)S(1)}, f32[512,128]{1,0:T(8,128)}, u32[]{:S(2)}) copy-start(f32[512,128]{1,0:T(8,128)} %get-tuple-element.5) | copy-start | bytes 786436

commit v2 on v1

v2 whole, which is shorter than its diff:
```python
import functools

import jax
import jax.numpy as jnp
import numpy as np
from jax import lax
from jax.experimental import pallas as pl
from jax.experimental.pallas import tpu as pltpu
from jax.sharding import PartitionSpec as P

EL_Y = 8
EL_Z = 16
MESH = pl.DeviceIdType.MESH
WIDEST = 32

spectrum_centre = 1.65
spectrum_half = 1.35


def legendre_table(positions, points):
    columns = [positions * 0.0 + 1.0, positions]
    for degree_now in range(2, points):
        columns.append(
            ((2 * degree_now - 1) * positions * columns[-1] - (degree_now - 1) * columns[-2])
            / degree_now
        )
    return np.stack(columns, axis=1)


def gll_derivative(points):
    degree = points - 1
    grid_nodes = -np.cos(np.pi * np.arange(points) / degree)
    for repeat in range(100):
        legendre = legendre_table(grid_nodes, points)
        grid_nodes = grid_nodes - (grid_nodes * legendre[:, degree] - legendre[:, degree - 1]) / (
            points * legendre[:, degree]
        )
    legendre = legendre_table(grid_nodes, points)
    top_values = legendre[:, degree]
    index_list = np.arange(points)
    same_index = index_list[:, None] == index_list[None, :]
    spacing = grid_nodes[:, None] - grid_nodes[None, :]
    spacing = np.where(same_index, 1.0, spacing)
    deriv_table = top_values[:, None] / (top_values[None, :] * spacing)
    deriv_table = np.where(same_index, 0.0, deriv_table)
    deriv_table[0, 0] = -degree * points / 4.0
    deriv_table[degree, degree] = degree * points / 4.0
    return deriv_table


def radices(count):
    factors = []
    while count > 1:
        width = max([w for w in range(2, WIDEST + 1) if count % w == 0], default=count)
        factors.append(width)
        count //= width
    return factors


def contract(values, table, symmetric):
    points = len(values)
    half = points // 2
    even = [values[j] + values[points - 1 - j] for j in range(half)]
    odd = [values[j] - values[points - 1 - j] for j in range(half)]
    low, high = [], []
    for m in range(half):
        a = [float(0.5 * (table[m, j] + table[m, points - 1 - j])) for j in range(half)]
        b = [float(0.5 * (table[m, j] - table[m, points - 1 - j])) for j in range(half)]
        part_even = a[0] * even[0]
        part_odd = b[0] * odd[0]
        for j in range(1, half):
            part_even = part_even + a[j] * even[j]
            part_odd = part_odd + b[j] * odd[j]
        low.append(part_even + part_odd)
        high.append(part_even - part_odd if symmetric else part_odd - part_even)
    return low + high[::-1]


def lane_gather(values, columns):
    dims = lax.GatherDimensionNumbers(
        offset_dims=(),
        collapsed_slice_dims=(1,),
        start_index_map=(1,),
        operand_batching_dims=(0,),
        start_indices_batching_dims=(0,),
    )
    return lax.gather(
        values, columns[..., None], dims, (1, 1), mode=lax.GatherScatterMode.PROMISE_IN_BOUNDS
    )


def kernel(
    count, points, factors, deriv,
    load_hbm, geo_hbm, mass_hbm, order_hbm, sol_ref, res_ref,
    load, geo, mass, start, inverse, vec, work, image,
    face_out, face_in, own_inv, near_inv, order, coef, sums, *rest,
):
    parts_in = rest[: len(factors)]
    (in_sem, face_send, face_recv, inv_sem, sum_send, sum_recv) = rest[len(factors):]
    me = lax.axis_index("slab")
    right = lax.rem(me + 1, count)
    left = lax.rem(me + count - 1, count)
    plane = points * points
    rows = points * plane
    last = rows - plane
    cols = load.shape[1]

    fetch = [
        pltpu.make_async_copy(geo_hbm, geo, in_sem.at[0]),
        pltpu.make_async_copy(mass_hbm, mass, in_sem.at[1]),
        pltpu.make_async_copy(load_hbm, load, in_sem.at[2]),
        pltpu.make_async_copy(order_hbm, order, in_sem.at[3]),
    ]
    for copy in fetch[::-1][:1] + fetch[:3]:
        copy.start()

    def peer(stride, width, k):
        digit = lax.rem(me // stride, width)
        return me + (lax.rem(digit + k, width) - digit) * stride

    strides = [int(np.prod(factors[:i])) for i in range(len(factors))]
    barrier = pltpu.get_barrier_semaphore()
    for near in (left, right):
        pl.semaphore_signal(barrier, inc=1, device_id=(near,), device_id_type=MESH)
    for stride, width in zip(strides, factors):
        @pl.loop(1, width)
        def _(k):
            pl.semaphore_signal(
                barrier, inc=1, device_id=(peer(stride, width, k),), device_id_type=MESH
            )

    fetch[3].wait()
    cell = order[...]
    cell8 = jnp.broadcast_to(cell, (points, cols))
    cell_col = jnp.transpose(jnp.broadcast_to(cell.astype(jnp.float32), (cols, cols)))
    lane = lax.broadcasted_iota(jnp.int32, (cols, cols), 1).astype(jnp.float32)
    source = lax.broadcasted_iota(jnp.int32, (cols, cols), 0).astype(jnp.float32)
    inv_row = jnp.sum(jnp.where(cell_col == lane, source, 0.0), axis=0, keepdims=True)
    inv8 = jnp.broadcast_to(inv_row.astype(jnp.int32), (points, cols))
    own_inv[...] = inv8
    pos_z = cell8 % EL_Z
    has_up = cell8 < cols - EL_Z
    has_down = cell8 >= EL_Z
    plus_y = lane_gather(inv8, jnp.where(has_up, cell8 + EL_Z, cell8))
    minus_y = lane_gather(inv8, jnp.where(has_down, cell8 - EL_Z, cell8))
    plus_z = lane_gather(inv8, jnp.where(pos_z == EL_Z - 1, cell8 - (EL_Z - 1), cell8 + 1))
    minus_z = lane_gather(inv8, jnp.where(pos_z == 0, cell8 + (EL_Z - 1), cell8 - 1))

    row_id = lax.broadcasted_iota(jnp.int32, (points, cols), 0)
    for t, table in enumerate((deriv, deriv.T, (deriv * deriv).T)):
        for k in range(points):
            vector = jnp.zeros((points, cols), jnp.float32)
            for m in range(points):
                vector = jnp.where(row_id == m, float(table[m, (m - k) % points]), vector)
            coef[t, k] = vector

    def rotate_contract(value, t):
        total = coef[t, 0] * value
        for k in range(1, points):
            total = total + coef[t, k] * pltpu.roll(value, k, 0)
        return total

    def send_pair(low_src, high_src, dst, send_sem, recv_sem):
        for src, side, near in ((low_src, 1, left), (high_src, 0, right)):
            pltpu.make_async_remote_copy(
                src_ref=src, dst_ref=dst.at[side], send_sem=send_sem, recv_sem=recv_sem,
                device_id=(near,), device_id_type=MESH,
            ).start()

    def settle(ref, send_sem, recv_sem):
        return pltpu.make_async_remote_copy(
            src_ref=ref, dst_ref=ref, send_sem=send_sem, recv_sem=recv_sem,
            device_id=(right,), device_id_type=MESH,
        )

    def send_faces(e):
        send_pair(face_out.at[e, 0], face_out.at[e, 1], face_in.at[e], face_send, face_recv.at[e])

    def wait_faces(e):
        settle(face_in.at[e], face_send, face_recv.at[e]).wait_recv()

    def at(base, b):
        return pl.ds(base + b * points, points)

    def geo_at(k, base, b):
        return pl.ds(k * rows + base + b * points, points)

    def store_face(e, side, b, value):
        face_out[e, side, pl.ds(b * points, points)] = value

    inner = [a * plane for a in range(1, points - 1)]

    def assemble_planes(spots):
        lows = [ref[at(base, 0)] for ref, base in spots]
        highs = [ref[at(base, points - 1)] for ref, base in spots]
        from_low = [lane_gather(low, plus_y) for low in lows]
        from_high = [lane_gather(high, minus_y) for high in highs]
        for i, (ref, base) in enumerate(spots):
            ref[at(base, points - 1)] = highs[i] + jnp.where(has_up, from_low[i], 0.0)
            ref[at(base, 0)] = lows[i] + jnp.where(has_down, from_high[i], 0.0)
        firsts = [pl.ds(base, points, stride=points) for _, base in spots]
        ends = [pl.ds(base + points - 1, points, stride=points) for _, base in spots]
        lows = [ref[first] for (ref, _), first in zip(spots, firsts)]
        highs = [ref[end] for (ref, _), end in zip(spots, ends)]
        from_low = [lane_gather(low, plus_z) for low in lows]
        from_high = [lane_gather(high, minus_z) for high in highs]
        for i, (ref, _) in enumerate(spots):
            ref[ends[i]] = highs[i] + from_low[i]
            ref[firsts[i]] = lows[i] + from_high[i]

    square = deriv * deriv
    fetch[0].wait()
    fetch[1].wait()

    for b in range(points):
        values = [geo[geo_at(0, a * plane, b)] for a in range(points)]
        for a, value in enumerate(contract(values, square.T, True)):
            work[at(a * plane, b)] = value

    def diagonal_plane(base, put):
        values = [geo[geo_at(1, base, b)] for b in range(points)]
        for b, value in enumerate(contract(values, square.T, True)):
            value = value + rotate_contract(geo[geo_at(2, base, b)], 2)
            put(b, value + work[at(base, b)] + mass[at(base, b)])

    diagonal_plane(0, functools.partial(store_face, 1, 0))
    diagonal_plane(last, functools.partial(store_face, 1, 1))
    pl.semaphore_wait(barrier, 2 + sum(w - 1 for w in factors))
    send_pair(
        load_hbm.at[pl.ds(0, plane)], load_hbm.at[pl.ds(last, plane)],
        face_in.at[0], face_send, face_recv.at[0],
    )
    send_pair(own_inv, own_inv, near_inv, inv_sem.at[0], inv_sem.at[1])
    send_faces(1)

    def first_update(base):
        for b in range(points):
            span = at(base, b)
            scaled = 1.0 / inverse[span]
            inverse[span] = scaled
            vec[span] = scaled * start[span] * (1.0 / spectrum_centre)

    fetch[2].wait()

    for base in inner:
        for b in range(points):
            start[at(base, b)] = load[at(base, b)]
    assemble_planes([(start, base) for base in inner])
    for base in inner:

        def put(b, value):
            inverse[at(base, b)] = value

        diagonal_plane(base, put)
    assemble_planes([(inverse, base) for base in inner])
    for base in inner:
        first_update(base)

    def along_first(put):
        for b in range(points):
            values = [vec[at(a * plane, b)] for a in range(points)]
            slopes = contract(values, deriv, False)
            fluxes = [geo[geo_at(0, a * plane, b)] * slopes[a] for a in range(points)]
            for a, value in enumerate(contract(fluxes, deriv.T, False)):
                put(a, b, value)

    def in_plane(base, ref):
        values = [vec[at(base, b)] for b in range(points)]
        slopes = contract(values, deriv, False)
        fluxes = [geo[geo_at(1, base, b)] * slopes[b] for b in range(points)]
        for b, value in enumerate(contract(fluxes, deriv.T, False)):
            flux = geo[geo_at(2, base, b)] * rotate_contract(values[b], 0)
            value = value + rotate_contract(flux, 1)
            ref[at(base, b)] = value + mass[at(base, b)] * values[b]

    def apply_faces_first(e, extra):
        for base in (0, last):
            in_plane(base, work)

        def put(a, b, term):
            span = at(a * plane, b)
            if a in (0, points - 1):
                out = work[span] + term
                store_face(e, int(a > 0), b, out)
            else:
                out = image[span] + term
                image[span] = out
            extra(span, out)

        along_first(put)
        send_faces(e)

    for base in inner:
        in_plane(base, image)

    settle(near_inv, inv_sem.at[0], inv_sem.at[1]).wait()
    minus_x = lane_gather(near_inv[0], cell8)
    plus_x = lane_gather(near_inv[1], cell8)

    def join_faces(e, own, ref):
        for side, (base, columns) in enumerate(((0, minus_x), (last, plus_x))):
            for b in range(points):
                ref[at(base, b)] = own(side, b) + lane_gather(
                    face_in[e, side, pl.ds(b * points, points)], columns
                )
        assemble_planes([(ref, 0), (ref, last)])

    def own_face(e):
        return lambda side, b: face_out[e, side, pl.ds(b * points, points)]

    wait_faces(0)
    join_faces(0, lambda side, b: load[at((0, last)[side], b)], start)
    wait_faces(1)
    join_faces(1, own_face(1), inverse)
    first_update(0)
    first_update(last)

    ratio_sigma = spectrum_centre / spectrum_half
    rho_prev = 1.0 / ratio_sigma
    rho_next = 1.0 / (2.0 * ratio_sigma - rho_prev)
    on_misfit = 2.0 * rho_next / spectrum_half
    on_start = (1.0 + rho_next * rho_prev) / spectrum_centre + on_misfit

    def second_update(base):
        for b in range(points):
            span = at(base, b)
            vec[span] = inverse[span] * (on_start * start[span] - on_misfit * image[span])

    apply_faces_first(2, lambda span, out: None)
    assemble_planes([(image, base) for base in inner])
    for base in inner:
        second_update(base)

    def sum_of(terms):
        while len(terms) > 1:
            terms = [x + y for x, y in zip(terms[::2], terms[1::2])] + terms[len(terms) & ~1:]
        return terms[0]

    def load_product(base):
        return sum_of([load[at(base, b)] * vec[at(base, b)] for b in range(points)])

    for base in inner:
        in_plane(base, image)
    on_load = sum_of([load_product(base) for base in inner])

    wait_faces(2)
    join_faces(2, own_face(2), image)
    second_update(0)
    second_update(last)

    products = []
    apply_faces_first(3, lambda span, out: products.append(vec[span] * out))
    on_load = on_load + load_product(0) + load_product(last)
    tally = [on_load, sum_of(products)]
    total = jnp.concatenate([jnp.sum(part, axis=0, keepdims=True) for part in tally], axis=1)

    def sum_copy(i, k):
        stride, width = strides[i], factors[i]
        return pltpu.make_async_remote_copy(
            src_ref=sums.at[i], dst_ref=parts_in[i].at[k - 1],
            send_sem=sum_send.at[i], recv_sem=sum_recv.at[i],
            device_id=(peer(stride, width, k),), device_id_type=MESH,
        )

    def start_sum(i, value):
        sums[i] = value

        @pl.loop(1, factors[i])
        def _(k):
            sum_copy(i, k).start()

    def finish_sum(i, value):
        settle(parts_in[i], sum_send.at[i], sum_recv.at[i]).wait()
        for k in range(factors[i] - 1):
            value = value + parts_in[i][k]
        return value

    start_sum(0, total)

    assemble_planes([(image, base) for base in inner])

    wait_faces(3)
    join_faces(3, own_face(3), image)
    for i in range(len(factors)):
        if i:
            start_sum(i, total)
        total = finish_sum(i, total)
    settle(face_out, face_send, face_recv.at[0]).wait_send()
    numerator = jnp.sum(total[:, :cols], axis=1, keepdims=True)
    denominator = jnp.sum(total[:, cols:], axis=1, keepdims=True)
    size = jnp.broadcast_to(numerator / denominator, (points, cols))

    for a in range(points):
        for b in range(points):
            span = at(a * plane, b)
            sol_ref[span] = size * vec[span]
            res_ref[span] = start[span] - size * image[span]


def on_device(count, load_terms, geometry, mass_terms, element_order):
    points = load_terms.shape[0]
    cols = load_terms.shape[3]
    plane = points * points
    rows = points * plane
    deriv = gll_derivative(points)
    factors = radices(count)
    f32 = jnp.float32
    big = [pltpu.VMEM((rows, cols), f32)]
    scratch = (
        big + [pltpu.VMEM((3 * rows, cols), f32)] + big * 6
        + [
            pltpu.VMEM((4, 2, plane, cols), f32),
            pltpu.VMEM((4, 2, plane, cols), f32),
            pltpu.VMEM((points, cols), jnp.int32),
            pltpu.VMEM((2, points, cols), jnp.int32),
            pltpu.VMEM((1, cols), jnp.int32),
            pltpu.VMEM((3, points, points, cols), f32),
            pltpu.VMEM((len(factors), 1, 2 * cols), f32),
        ]
        + [pltpu.VMEM((w - 1, 1, 2 * cols), f32) for w in factors]
        + [
            pltpu.SemaphoreType.DMA((4,)),
            pltpu.SemaphoreType.DMA,
            pltpu.SemaphoreType.DMA((4,)),
            pltpu.SemaphoreType.DMA((2,)),
            pltpu.SemaphoreType.DMA((len(factors),)),
            pltpu.SemaphoreType.DMA((len(factors),)),
        ]
    )
    hbm = pl.BlockSpec(memory_space=pl.ANY)
    vmem = pl.BlockSpec(memory_space=pltpu.VMEM)
    solution_rows, residual_rows = pl.pallas_call(
        functools.partial(kernel, count, points, factors, deriv),
        out_shape=(pltpu.VMEM((rows, cols), f32),) * 2,
        in_specs=[hbm] * 4,
        out_specs=(vmem, vmem),
        scratch_shapes=scratch,
        compiler_params=pltpu.CompilerParams(collective_id=0, has_side_effects=True),
    )(
        load_terms.reshape(rows, cols),
        geometry.reshape(3 * rows, cols),
        mass_terms.reshape(rows, cols),
        element_order,
    )
    shape = load_terms.shape
    return solution_rows.reshape(shape), residual_rows.reshape(shape)


def solution(mesh):
    placed = (
        P(None, None, None, "slab"),
        P(None, None, None, None, "slab"),
        P(None, None, None, "slab"),
        P("slab", None),
    )
    return jax.shard_map(
        functools.partial(on_device, mesh.shape["slab"]),
        mesh=mesh,
        in_specs=placed,
        out_specs=(P(None, None, None, "slab"), P(None, None, None, "slab")),
        check_vma=False,
    )
```

time: 25.5 us -> 22.4 us (0.88)
  Pallas kernels: 22.3 us -> 20.2 us
  local copies, waits for them, and re-layouts: 2.42 us -> 1.41 us
    pallas_call x1, Pallas kernels: 22.3 us -> 20.2 us  [on_device(): pl.pallas_call(functools.partial(kernel, count, points, factors, deriv),...]
    unnamed x4 -> x2, local copies, waits for them, and re-layouts: 2.42 us -> 1.41 us
where the time goes in v2:
time: 22.4 us; the launch traced here: 22.3 us
  Pallas kernels  20.2 us (90%)
  local copies, waits for them, and re-layouts  1.41 us (6%)
  between operations  0.64 us (3%)
    pallas_call x1, Pallas kernels, on_device(): pl.pallas_call(functools.partial(kernel, count, points, factors, deriv),...  20.2 us
    unnamed x2, local copies, waits for them, and re-layouts  1.41 us

profile of v2, /device:TPU:0, one launch (start us, length us, event | category | flops | bytes accessed | tf_op | source)
XLA Modules:
  0.0 22.3 jit_solution(16661349491252742893)
XLA Ops:
  0.6 20.2 %shard_map.59 = (f32[512,128]{1,0:T(8,128)S(1)}, f32[512,128]{1,0:T(8,128)S(1)}) custom-call(f32[512,128]{1,0:T(8,128)} %bitcast.8, f32[1536,128]{1,0:T(8,128)} %bitcast.7, f32[512,128]{1,0:T(8,128)} %bitcast.9, s32[1,128]{1,0:T(1,128)} %order_hbm.1), custom_call_target="tpu_custom_call" | custom-call | tf_op jit(solution)/shard_map/pallas_call | solution.py:432
  20.9 0.7 %copy.8 = f32[8,8,8,128]{3,2,1,0:T(8,128)} copy(f32[8,8,8,128]{3,2,1,0:T(8,128)S(1)} %bitcast.6) | data formatting | bytes 524288
  21.6 0.7 %copy.9 = f32[8,8,8,128]{3,2,1,0:T(8,128)} copy(f32[8,8,8,128]{3,2,1,0:T(8,128)S(1)} %bitcast.5) | data formatting | bytes 524288
